TPU v7x, 256 devices: a whole 4x4x8 slice. The times are simulated.
256 devices in a mesh: dp: 16 (over z_lo, x), seq: 16 (over z_hi, y, core).
Axes of the slice: x: 4, y: 4, z: 8 (z_hi: 2, z_lo: 4; z = z_hi * 4 + z_lo), core: 2. Of those that a mesh axis runs over, the one named last changes fastest.
Arguments:
- frames: bfloat16 [16, 4096, 1280], P('dp', 'seq'), may hold values from -6 to 6
- live: int32 [16, 4096], P('dp', 'seq'), may hold values from 0 to 1
- norm_gain: float32 [1280], replicated, may hold values from 0.25 to 1.75
- w_qkv: bfloat16 [1280, 1920], P('dp')
- w_out: bfloat16 [640, 1280], P('dp'), may hold values from -0.25 to 0.25
- cotangent: bfloat16 [16, 4096, 1280], P('dp', 'seq'), may hold values from -6 to 6
Outputs:
- grad_frames: bfloat16 [16, 4096, 1280], P('dp', 'seq')
- grad_qkv: float32 [1280, 1920], P('dp', 'seq')
- grad_out: float32 [640, 1280], P('dp', 'seq')
All inputs are finite; a program needn't handle non-finite values.
Results may differ from a plain program's by a relative error of at most 0.0095.
Values may be sent and summed in bfloat16 or wider, within the bound.
No kernel may reach another device: no remote copies, remote signals or barrier semaphores. Data moves between devices by JAX's collectives and lax.ppermute only.
A program may use at most 64 MiB of HBM per device.

v0:
```python
import math
import jax
import jax.numpy as jnp
from jax import lax
from jax.sharding import PartitionSpec as P

HEAD_DIM = 64
WIN = 512
EPS = 1e-05
NEG = -1e30


def from_behind(value, axis, steps):
    count = lax.axis_size(axis)
    leading, last = (max(0, -steps), min(count, count - steps))
    return lax.ppermute(value, axis, [(source, source + steps) for source in range(leading, last)])


def norm_rows(values_in):
    average = jnp.mean(values_in, axis=-1, keepdims=True)
    centred = values_in - average
    inverse = lax.rsqrt(jnp.mean(centred * centred, axis=-1, keepdims=True) + EPS)
    return (centred * inverse, inverse)


def against(left, right):
    return lax.dot_general(
        left, right, (((1,), (1,)), ((), ())), preferred_element_type=jnp.float32
    )


def leading(left, right):
    return lax.dot_general(
        left, right, (((0,), (0,)), ((), ())), preferred_element_type=jnp.float32
    )


def head_terms(query_head, key_head, value_head, grad_head, allowed, query_live, score_scale):
    scores = jnp.where(allowed, against(query_head, key_head) * score_scale, NEG)
    row_peak = jnp.max(scores, axis=-1, keepdims=True)
    exponent = jnp.exp(scores - row_peak)
    probabilities = exponent / jnp.sum(exponent, axis=-1, keepdims=True)
    probs_b = probabilities.astype(jnp.bfloat16)
    mixed = jnp.dot(probs_b, value_head, preferred_element_type=jnp.float32) * query_live[:, None]
    attended = mixed.astype(jnp.bfloat16)
    row_delta = jnp.sum(grad_head.astype(jnp.float32) * attended.astype(jnp.float32), axis=1)
    grad_probs = against(grad_head, value_head)
    grad_scores = (probabilities * (grad_probs - row_delta[:, None]) * score_scale).astype(
        jnp.bfloat16
    )
    grad_query = jnp.dot(grad_scores, key_head, preferred_element_type=jnp.float32)
    grad_key = leading(grad_scores, query_head)
    grad_value = leading(probs_b, grad_head)
    return (attended, grad_query, grad_key, grad_value)


def body(frames, live, norm_gain, w_qkv, w_out, cotangent):
    length = frames.shape[1]
    n_data = lax.axis_size("dp")
    n_seq = lax.axis_size("seq")
    full_qkv, full_out = (
        lax.all_gather(w_qkv, "dp", axis=0, tiled=True),
        lax.all_gather(w_out, "dp", axis=0, tiled=True),
    )
    inner = full_out.shape[0]
    heads = inner // HEAD_DIM
    hidden = frames[0].astype(jnp.float32)
    unit_rows, inverse = norm_rows(hidden)
    normed = (unit_rows * norm_gain).astype(jnp.bfloat16)
    projected = jnp.dot(normed, full_qkv, preferred_element_type=jnp.float32).astype(jnp.bfloat16)
    query = projected[:, :inner]
    key_values = projected[:, inner:]
    live_row = live[0]
    query_live = live_row.astype(jnp.float32)
    live_mark = live_row.astype(jnp.bfloat16)
    upstream = cotangent[0]
    grad_att = (against(upstream, full_out) * query_live[:, None]).astype(jnp.bfloat16)
    neighbours = -(-WIN // length)
    offsets = list(range(neighbours, 0, -1)) + list(range(-1, -neighbours - 1, -1))
    before_pairs, before_marks, after_pairs, after_marks = ([], [], [], [])
    for offset in offsets:
        distance = abs(offset)
        row_count = min(length, WIN - (distance - 1) * length)
        if offset > 0:
            send_pairs = key_values
            send_marks = live_mark
        else:
            send_pairs = key_values
            send_marks = live_mark
        got_pairs, got_marks = from_behind((send_pairs, send_marks), "seq", offset)
        if offset > 0:
            before_pairs.append(got_pairs)
            before_marks.append(got_marks)
        else:
            after_pairs.append(got_pairs)
            after_marks.append(got_marks)
    ext_pairs = jnp.concatenate(before_pairs + [key_values] + after_pairs, axis=0)
    ext_live = jnp.concatenate(before_marks + [live_mark] + after_marks, axis=0).astype(jnp.float32)
    total_span = length + 2 * WIN
    block_rows = min(length, 512)
    key_span = block_rows + 2 * WIN
    query_pos = jnp.arange(block_rows, dtype=jnp.int32)
    key_pos = jnp.arange(key_span, dtype=jnp.int32) - WIN
    in_window = jnp.abs(query_pos[:, None] - key_pos[None, :]) <= WIN
    allowances = [in_window & (ext_live[None, :] > 0.5)]
    score_scale = 1.0 / math.sqrt(HEAD_DIM)

    def split_heads(matrix):
        return matrix.reshape(matrix.shape[0], heads, HEAD_DIM).transpose(1, 0, 2)

    def merge_heads(matrix):
        return matrix.transpose(1, 0, 2).reshape(matrix.shape[1], inner)

    def one_head(inputs):
        query_head, key_head, value_head, grad_head = inputs
        out_blocks, query_blocks = ([], [])
        key_grads = jnp.zeros((total_span, HEAD_DIM), jnp.float32)
        value_grads = jnp.zeros((total_span, HEAD_DIM), jnp.float32)
        attended, grad_query, grad_key, grad_value = head_terms(
            query_head, key_head, value_head, grad_head, allowances[0], query_live, score_scale
        )
        out_blocks.append(attended)
        query_blocks.append(grad_query)
        key_grads = key_grads.at[0:key_span].add(grad_key)
        value_grads = value_grads.at[0:key_span].add(grad_value)
        return (
            jnp.concatenate(out_blocks, axis=0),
            jnp.concatenate(query_blocks, axis=0),
            key_grads,
            value_grads,
        )

    att_heads, query_heads, key_heads, value_heads = lax.map(
        one_head,
        (
            split_heads(query),
            split_heads(ext_pairs[:, :inner]),
            split_heads(ext_pairs[:, inner:]),
            split_heads(grad_att),
        ),
    )
    attention = merge_heads(att_heads)
    grad_query = merge_heads(query_heads)
    ext_grads = jnp.concatenate([merge_heads(key_heads), merge_heads(value_heads)], axis=1)
    own_grads = ext_grads[WIN : WIN + length]
    for offset in offsets:
        distance = abs(offset)
        row_count = min(length, WIN - (distance - 1) * length)
        if offset > 0:
            first_row = WIN - distance * length + length - row_count
        else:
            first_row = WIN + length + (distance - 1) * length
        arrived = from_behind(ext_grads[first_row : first_row + row_count], "seq", -offset)
        if offset > 0:
            own_grads = own_grads.at[length - row_count :].add(arrived)
        else:
            own_grads = own_grads.at[:row_count].add(arrived)
    grad_projected = jnp.concatenate([grad_query, own_grads], axis=1).astype(jnp.bfloat16)
    grad_unit = against(grad_projected, full_qkv) * norm_gain
    through = inverse * (
        grad_unit
        - jnp.mean(grad_unit, axis=-1, keepdims=True)
        - unit_rows * jnp.mean(grad_unit * unit_rows, axis=-1, keepdims=True)
    )
    grad_rows = (upstream.astype(jnp.float32) + through).astype(jnp.bfloat16)[None]
    factor = 1.0 / math.sqrt(n_data * n_seq * length)
    term_qkv = leading(normed, grad_projected)
    term_out = leading(attention, upstream)
    part_qkv, part_out = (
        lax.psum_scatter(term_qkv, "seq", scatter_dimension=1, tiled=True),
        lax.psum_scatter(term_out, "seq", scatter_dimension=1, tiled=True),
    )
    sum_qkv, sum_out = (
        lax.psum_scatter(part_qkv, "dp", scatter_dimension=0, tiled=True),
        lax.psum_scatter(part_out, "dp", scatter_dimension=0, tiled=True),
    )
    return (grad_rows, sum_qkv * factor, sum_out * factor)


def solution(mesh):
    return jax.shard_map(
        body,
        mesh=mesh,
        in_specs=(
            P("dp", "seq", None),
            P("dp", "seq"),
            P(),
            P("dp", None),
            P("dp", None),
            P("dp", "seq", None),
        ),
        out_specs=(P("dp", "seq", None), P("dp", "seq"), P("dp", "seq")),
        check_vma=False,
    )
```

profile of v0, /device:TPU:8, one launch (start us, length us, event | category | flops | bytes accessed | tf_op | source)
XLA Modules:
  0.0 898.2 jit_solution(4358646345607529689)
XLA Ops:
  9.4 3.5 collective-permute-start.4
  14.8 3.6 collective-permute-start.6
  22.0 79.7 %all-gather.3.cloned.1.call-done = bf16[1280,1920]{1,0:T(8,128)(2,1)} async-done(((bf16[80,1920]{1,0:T(8,128)(2,1)}), bf16[1280,1920]{1,0:T(8,128)(2,1)}) %all-gather.3.cloned.1.call-update) | async-done | bytes 4915216 | tf_op jit(solution)/shard_map/all_gather | solution.py:62
  101.7 4.0 convolution_convert_fusion
  107.6 3.3 collective-permute-start
  113.9 70.7 %all-gather.5.cloned.1.call-done = bf16[640,1280]{1,0:T(8,128)(2,1)} async-done(((bf16[40,1280]{1,0:T(8,128)(2,1)}), bf16[640,1280]{1,0:T(8,128)(2,1)}) %all-gather.5.cloned.1.call-update) | async-done | bytes 1638416 | tf_op jit(solution)/shard_map/all_gather | solution.py:63
  199.4 5.4 collective-permute-done.2
  206.0 9.9 %collective-permute-done.3 = bf16[256,1280]{1,0:T(8,128)(2,1)} collective-permute-done((bf16[256,1280]{1,0:T(8,128)(2,1)}, bf16[256,1280]{1,0:T(8,128)(2,1)}, u32[]{:S(2)}, u32[]{:S(2)}) %collective-permute-start.3) | collective-permute-done | bytes 655392 | tf_op jit(solution)/shard_map/ppermute | solution.py:16
  219.0 3.6 copy.25
  222.6 3.5 copy.26
  226.1 109.6 %while.32 = (s32[]{:T(128)}, bf16[10,256,64]{1,2,0:T(8,128)(2,1)}, bf16[10,256,64]{1,2,0:T(8,128)(2,1)}, f32[10,1280,64]{1,2,0:T(8,128)S(1)}, f32[10,1280,64]{1,...) while((s32[]{:T(128)}, bf16[10,256,64]{1,2,0:T(8,128)(2,1)}, ...), condition=%wide.region_6.7_spmd.clone, body=%wide.region_2.6_spmd.clone.sunk | while | flops 258637056 | bytes 10183041 | solution.py:133
  335.7 3.6 fusion.63
  343.6 8.6 collective-permute-start.11
  354.2 3.1 collective-permute-start.9
  357.3 14.8 %collective-permute-done.10 = f32[256,1280]{0,1:T(8,128)S(1)} collective-permute-done((f32[256,1280]{0,1:T(8,128)S(1)}, f32[256,1280]{0,1:T(8,128)S(1)}, u32[]{:S(2)}, u32[]{:S(2)}) %collective-permute-start.10) | collective-permute-done | bytes 1310752 | tf_op jit(solution)/shard_map/ppermute | solution.py:16
  372.1 9.2 %collective-permute-done.11 = f32[256,1280]{0,1:T(8,128)S(1)} collective-permute-done((f32[256,1280]{0,1:T(8,128)S(1)}, f32[256,1280]{0,1:T(8,128)S(1)}, u32[]{:S(2)}, u32[]{:S(2)}) %collective-permute-start.11) | collective-permute-done | bytes 1310752 | tf_op jit(solution)/shard_map/ppermute | solution.py:16
  381.4 4.1 collective-permute-done.8
  385.5 14.1 %collective-permute-done.9 = f32[256,1280]{0,1:T(8,128)S(1)} collective-permute-done((f32[256,1280]{0,1:T(8,128)S(1)}, f32[256,1280]{0,1:T(8,128)S(1)}, u32[]{:S(2)}, u32[]{:S(2)}) %collective-permute-start.9) | collective-permute-done | bytes 1310752 | tf_op jit(solution)/shard_map/ppermute | solution.py:16
  400.8 5.3 fusion.66
  406.3 88.3 %reduce-scatter.9.cloned.1.call-done = f32[640,80]{0,1:T(8,128)} async-done(((f32[640,1280]{0,1:T(8,128)}), f32[640,80]{0,1:T(8,128)}) %reduce-scatter.9.cloned.1.call-update) | async-done | bytes 204816 | tf_op jit(solution)/shard_map/reduce_scatter | solution.py:171
  495.8 153.3 %reduce-scatter.7.cloned.1.call-done = f32[1280,120]{0,1:T(8,128)} async-done(((f32[1280,1920]{0,1:T(8,128)}), f32[1280,120]{0,1:T(8,128)}) %reduce-scatter.7.cloned.1.call-update) | async-done | bytes 614416 | tf_op jit(solution)/shard_map/reduce_scatter | solution.py:170
  651.4 4.2 fusion.71
  657.0 146.1 %all-reduce.3.cloned.1.call-done = f32[640,80]{0,1:T(8,128)} async-done(((f32[640,80]{0,1:T(8,128)}), f32[640,80]{0,1:T(8,128)}) %all-reduce.3.cloned.1.call-update) | async-done | bytes 204816
  804.8 85.0 %reduce-scatter.11.cloned.1.call-done = f32[80,120]{1,0:T(8,128)} async-done(((f32[1280,120]{1,0:T(8,128)}), f32[80,120]{1,0:T(8,128)}) %reduce-scatter.11.cloned.1.call-update) | async-done | bytes 38416
  (173 shorter events, 155.9 us)
Async XLA Ops:
  7.2 94.5 %copy-start.11 = (f32[1280]{0:T(1024)S(1)}, f32[1280]{0:T(1024)}, u32[]{:S(2)}) copy-start(f32[1280]{0:T(1024)} %param.34) | copy-start | bytes 15364
  7.2 94.5 %all-gather.3.cloned.1.call-start = ((), (), s32[]{:S(2)}) async-start(), calls=%async_computation.3 | async-start | bytes 5222400 | tf_op jit(solution)/shard_map/all_gather | solution.py:62
  7.9 176.6 %all-gather.5.cloned.1.call-start = ((), (), s32[]{:S(2)}) async-start(), calls=%async_computation.4 | async-start | bytes 1740800 | tf_op jit(solution)/shard_map/all_gather | solution.py:63
  8.7 485.8 %reduce-scatter.9.cloned.1.call-start = ((), (), s32[]{:S(2)}) async-start(), calls=%async_computation.6 | async-start | bytes 3481600 | tf_op jit(solution)/shard_map/reduce_scatter | solution.py:171
  9.4 101.6 %collective-permute-start.4 = (bf16[256]{0:T(256)(128)(2,1)S(1)}, bf16[256]{0:T(256)(128)(2,1)S(1)}, u32[]{:S(2)}, u32[]{:S(2)}) collective-permute-start(bf16[256]{0:T(256)(128)(2,1)S(1)} %convert_reduce_fusion.1), channel_id=1, source_target_pairs={{0,2},{1,3},{2,4},{3,5},{4,6},{5,7},{6,8},{7,9},{8,10},{9,11},{10,... | collective-permute-start | bytes 1544 | tf_op jit(solution)/shard_map/ppermute | solution.py:16
  12.9 98.4 %collective-permute-start.5 = (bf16[256]{0:T(256)(128)(2,1)S(1)}, bf16[256]{0:T(256)(128)(2,1)S(1)}, u32[]{:S(2)}, u32[]{:S(2)}) collective-permute-start(bf16[256]{0:T(256)(128)(2,1)S(1)} %convert_reduce_fusion.1), channel_id=1, source_target_pairs={{0,1},{1,2},{2,3},{3,4},{4,5},{5,6},{6,7},{7,8},{8,9},{9,10},{10,1... | collective-permute-start | bytes 1544 | tf_op jit(solution)/shard_map/ppermute | solution.py:16
  14.8 96.9 %collective-permute-start.6 = (bf16[256]{0:T(256)(128)(2,1)S(1)}, bf16[256]{0:T(256)(128)(2,1)S(1)}, u32[]{:S(2)}, u32[]{:S(2)}) collective-permute-start(bf16[256]{0:T(256)(128)(2,1)S(1)} %convert_reduce_fusion.1), channel_id=1, source_target_pairs={{1,0},{2,1},{3,2},{4,3},{5,4},{6,5},{7,6},{8,7},{9,8},{10,9},{11,1... | collective-permute-start | bytes 1544 | tf_op jit(solution)/shard_map/ppermute | solution.py:16
  18.5 93.4 %collective-permute-start.7 = (bf16[256]{0:T(256)(128)(2,1)S(1)}, bf16[256]{0:T(256)(128)(2,1)S(1)}, u32[]{:S(2)}, u32[]{:S(2)}) collective-permute-start(bf16[256]{0:T(256)(128)(2,1)S(1)} %convert_reduce_fusion.1), channel_id=1, source_target_pairs={{2,0},{3,1},{4,2},{5,3},{6,4},{7,5},{8,6},{9,7},{10,8},{11,9},{12,... | collective-permute-start | bytes 1544 | tf_op jit(solution)/shard_map/ppermute | solution.py:16
  107.6 89.4 %collective-permute-start = (bf16[256,1280]{1,0:T(8,128)(2,1)}, bf16[256,1280]{1,0:T(8,128)(2,1)}, u32[]{:S(2)}, u32[]{:S(2)}) collective-permute-start(bf16[256,1280]{1,0:T(8,128)(2,1)} %slice.121), channel_id=1, source_target_pairs={{0,2},{1,3},{2,4},{3,5},{4,6},{5,7},{6,8},{7,9},{8,10},{9,11},{10,... | collective-permute-start | bytes 1966088 | tf_op jit(solution)/shard_map/ppermute | solution.py:16
  111.9 86.3 %collective-permute-start.1 = (bf16[256,1280]{1,0:T(8,128)(2,1)}, bf16[256,1280]{1,0:T(8,128)(2,1)}, u32[]{:S(2)}, u32[]{:S(2)}) collective-permute-start(bf16[256,1280]{1,0:T(8,128)(2,1)} %slice.121), channel_id=1, source_target_pairs={{0,1},{1,2},{2,3},{3,4},{4,5},{5,6},{6,7},{7,8},{8,9},{9,10},{10,1... | collective-permute-start | bytes 1966088 | tf_op jit(solution)/shard_map/ppermute | solution.py:16
  189.5 15.3 %collective-permute-start.2 = (bf16[256,1280]{1,0:T(8,128)(2,1)}, bf16[256,1280]{1,0:T(8,128)(2,1)}, u32[]{:S(2)}, u32[]{:S(2)}) collective-permute-start(bf16[256,1280]{1,0:T(8,128)(2,1)} %slice.121), channel_id=1, source_target_pairs={{1,0},{2,1},{3,2},{4,3},{5,4},{6,5},{7,6},{8,7},{9,8},{10,9},{11,1... | collective-permute-start | bytes 1966088 | tf_op jit(solution)/shard_map/ppermute | solution.py:16
  191.4 24.4 %collective-permute-start.3 = (bf16[256,1280]{1,0:T(8,128)(2,1)}, bf16[256,1280]{1,0:T(8,128)(2,1)}, u32[]{:S(2)}, u32[]{:S(2)}) collective-permute-start(bf16[256,1280]{1,0:T(8,128)(2,1)} %slice.121), channel_id=1, source_target_pairs={{2,0},{3,1},{4,2},{5,3},{6,4},{7,5},{8,6},{9,7},{10,8},{11,9},{12,... | collective-permute-start | bytes 1966088 | tf_op jit(solution)/shard_map/ppermute | solution.py:16
  339.4 309.8 %reduce-scatter.7.cloned.1.call-start = ((), (), s32[]{:S(2)}) async-start(), calls=%async_computation.5 | async-start | bytes 10444800 | tf_op jit(solution)/shard_map/reduce_scatter | solution.py:170
  339.4 60.1 %copy-start = (f32[10,1280,64]{1,2,0:T(8,128)S(1)}, f32[10,1280,64]{1,2,0:T(8,128)}, u32[]{:S(2)}) copy-start(f32[10,1280,64]{1,2,0:T(8,128)} %get-tuple-element.301) | copy-start | bytes 9830404
  341.6 30.5 %collective-permute-start.10 = (f32[256,1280]{0,1:T(8,128)S(1)}, f32[256,1280]{0,1:T(8,128)S(1)}, u32[]{:S(2)}, u32[]{:S(2)}) collective-permute-start(f32[256,1280]{0,1:T(8,128)S(1)} %get-tuple-element.397), channel_id=1, source_target_pairs={{0,1},{1,2},{2,3},{3,4},{4,5},{5,6},{6,7},{7,8},{8,9},{9,10},{10,1... | collective-permute-start | bytes 3932168 | tf_op jit(solution)/shard_map/ppermute | solution.py:16
  343.6 37.8 %collective-permute-start.11 = (f32[256,1280]{0,1:T(8,128)S(1)}, f32[256,1280]{0,1:T(8,128)S(1)}, u32[]{:S(2)}, u32[]{:S(2)}) collective-permute-start(f32[256,1280]{0,1:T(8,128)S(1)} %get-tuple-element.396), channel_id=1, source_target_pairs={{0,2},{1,3},{2,4},{3,5},{4,6},{5,7},{6,8},{7,9},{8,10},{9,11},{10,... | collective-permute-start | bytes 3932168 | tf_op jit(solution)/shard_map/ppermute | solution.py:16
  352.2 33.3 %collective-permute-start.8 = (f32[256,1280]{0,1:T(8,128)S(1)}, f32[256,1280]{0,1:T(8,128)S(1)}, u32[]{:S(2)}, u32[]{:S(2)}) collective-permute-start(f32[256,1280]{0,1:T(8,128)S(1)} %get-tuple-element.394), channel_id=1, source_target_pairs={{2,0},{3,1},{4,2},{5,3},{6,4},{7,5},{8,6},{9,7},{10,8},{11,9},{12,... | collective-permute-start | bytes 3932168 | tf_op jit(solution)/shard_map/ppermute | solution.py:16
  354.2 45.4 %collective-permute-start.9 = (f32[256,1280]{0,1:T(8,128)S(1)}, f32[256,1280]{0,1:T(8,128)S(1)}, u32[]{:S(2)}, u32[]{:S(2)}) collective-permute-start(f32[256,1280]{0,1:T(8,128)S(1)} %get-tuple-element.395), channel_id=1, source_target_pairs={{1,0},{2,1},{3,2},{4,3},{5,4},{6,5},{7,6},{8,7},{9,8},{10,9},{11,1... | collective-permute-start | bytes 3932168 | tf_op jit(solution)/shard_map/ppermute | solution.py:16
  406.1 88.4 %copy-start.13 = (u32[256]{0:T(256)S(1)}, u32[256]{0:T(256)}, u32[]{:S(2)}) copy-start(u32[256]{0:T(256)} %constant.302) | copy-start | bytes 3076
  406.2 245.2 %copy-start.3 = (bf16[1,256,1280]{2,1,0:T(8,128)(2,1)S(1)}, bf16[1,256,1280]{2,1,0:T(8,128)(2,1)}, u32[]{:S(2)}) copy-start(bf16[1,256,1280]{2,1,0:T(8,128)(2,1)} %param.32) | copy-start | bytes 1966084
  406.2 245.2 %copy-start.7 = (bf16[256,1280]{0,1:T(8,128)(2,1)S(1)}, bf16[256,1280]{0,1:T(8,128)(2,1)}, u32[]{:S(2)}) copy-start(bf16[256,1280]{0,1:T(8,128)(2,1)} %copy-done.6) | copy-start | bytes 1966084
  406.2 245.2 %copy-start.10 = (bf16[10,256,64]{1,2,0:T(8,128)(2,1)S(1)}, bf16[10,256,64]{1,2,0:T(8,128)(2,1)}, u32[]{:S(2)}) copy-start(bf16[10,256,64]{1,2,0:T(8,128)(2,1)} %get-tuple-element.299) | copy-start | bytes 983044
  406.2 396.9 %all-reduce.3.cloned.1.call-start = ((), (), s32[]{:S(2)}) async-start(), calls=%async_computation.8 | async-start | bytes 409600
  494.5 395.2 %reduce-scatter.11.cloned.1.call-start = ((), (), s32[]{:S(2)}) async-start(), calls=%async_computation.7 | async-start | bytes 696320
  (8 other events, 120.5 us)
Sparse Core Ops, SparseCore 0:
  9.8 91.8 all-gather.2
  103.5 81.0 all-gather.4
  339.5 155.0 reduce-scatter.8
  499.1 149.9 reduce-scatter.6
  651.6 151.4 all-reduce.2
  805.5 84.2 reduce-scatter.10
where the time goes:
time: 902 us; the launch traced here: 898 us
  waiting for transfers between devices  682 us (76%)
  matrix products  118 us (13%)
  starting transfers between devices  35.9 us (4%)
  local copies, waits for them, and re-layouts  27.9 us (3%)
  other arithmetic  18.6 us (2%)
  between operations  15.2 us (2%)
    unnamed x8, waiting for transfers between devices  233 us
    reduce_scatter x1, waiting for transfers between devices, body(): lax.psum_scatter(term_qkv, 'seq', scatter_dimension=1, tiled=True)  153 us
    reduce_scatter x1, waiting for transfers between devices, body(): lax.psum_scatter(term_out, 'seq', scatter_dimension=1, tiled=True)  88.3 us
    all_gather x1, waiting for transfers between devices, body(): lax.all_gather(w_qkv, 'dp', axis=0, tiled=True)  79.7 us
    all_gather x1, waiting for transfers between devices, body(): lax.all_gather(w_out, 'dp', axis=0, tiled=True)  70.7 us
    ppermute x12, waiting for transfers between devices, from_behind(): lax.ppermute(value, axis, [(source, source + steps) for source in range(l...  57.6 us
    dot_general x22, matrix products, against(): lax.dot_general(left, right, (((1,), (1,)), ((), ())), preferred_element_...  38 us
    dot_general x22, matrix products, leading(): lax.dot_general(left, right, (((0,), (0,)), ((), ())), preferred_element_...  38 us
  transfers between devices with their start and end apart: 18, of which 12 were waited for; matrix products, arithmetic and copies ran while one was open for 4% of the time, Pallas kernels for 0%

commit v1 on v0

--- a/solution.py
+++ b/solution.py
@@ -58,10 +58,20 @@
     length = frames.shape[1]
     n_data = lax.axis_size("dp")
     n_seq = lax.axis_size("seq")
-    full_qkv, full_out = (
-        lax.all_gather(w_qkv, "dp", axis=0, tiled=True),
-        lax.all_gather(w_out, "dp", axis=0, tiled=True),
-    )
+
+    def apply_the_view(block_here):
+        h_now = jnp.concatenate(
+            lax.all_to_all(
+                jnp.stack(tuple((block_here for _ in range(lax.axis_size("dp")))), 0),
+                axis_name="dp",
+                split_axis=0,
+                concat_axis=0,
+            ),
+            0,
+        )
+        return h_now
+
+    full_qkv, full_out = (apply_the_view(w_qkv), lax.all_gather(w_out, "dp", axis=0, tiled=True))
     inner = full_out.shape[0]
     heads = inner // HEAD_DIM
     hidden = frames[0].astype(jnp.float32)

time: 902 us -> 894 us (level)
  waiting for transfers between devices: 682 us -> 665 us
    all_to_all x0 -> x1, waiting for transfers between devices: none -> 96.4 us  [apply_the_view(): lax.all_to_all(jnp.stack(tuple((block_here for _ in range(lax.axis_size('...]
    all_gather x1 -> x0, waiting for transfers between devices: 79.7 us -> none  [body(): lax.all_gather(w_qkv, 'dp', axis=0, tiled=True)]
    all_gather x1, waiting for transfers between devices: 70.7 us -> 0.02 us  [body(): lax.all_gather(w_out, 'dp', axis=0, tiled=True)]
    reduce_scatter x1, waiting for transfers between devices: 88.3 us -> 128 us  [body(): lax.psum_scatter(term_out, 'seq', scatter_dimension=1, tiled=True)]
    unnamed x8 -> x7, waiting for transfers between devices: 233 us -> 232 us
where the time goes in v1:
time: 894 us; the launch traced here: 890 us
  waiting for transfers between devices  665 us (74%)
  matrix products  119 us (13%)
  starting transfers between devices  43.7 us (5%)
  local copies, waits for them, and re-layouts  31.4 us (4%)
  other arithmetic  16.9 us (2%)
  between operations  14.8 us (2%)
    unnamed x7, waiting for transfers between devices  232 us
    reduce_scatter x1, waiting for transfers between devices, body(): lax.psum_scatter(term_qkv, 'seq', scatter_dimension=1, tiled=True)  154 us
    reduce_scatter x1, waiting for transfers between devices, body(): lax.psum_scatter(term_out, 'seq', scatter_dimension=1, tiled=True)  128 us
    all_to_all x1, waiting for transfers between devices, apply_the_view(): lax.all_to_all(jnp.stack(tuple((block_here for _ in range(lax.axis_size('...  96.4 us
    ppermute x12, waiting for transfers between devices, from_behind(): lax.ppermute(value, axis, [(source, source + steps) for source in range(l...  55.2 us
    dot_general x22, matrix products, against(): lax.dot_general(left, right, (((1,), (1,)), ((), ())), preferred_element_...  38 us
    dot_general x22, matrix products, leading(): lax.dot_general(left, right, (((0,), (0,)), ((), ())), preferred_element_...  38 us
    ppermute x12, starting transfers between devices, from_behind(): lax.ppermute(value, axis, [(source, source + steps) for source in range(l...  34.9 us
  transfers between devices with their start and end apart: 18, of which 12 were waited for; matrix products, arithmetic and copies ran while one was open for 4% of the time, Pallas kernels for 0%

profile of v1, /device:TPU:8, one launch (start us, length us, event | category | flops | bytes accessed | tf_op | source)
XLA Modules:
  0.0 890.3 jit_solution(14534896186449436055)
XLA Ops:
  7.2 3.5 stack.2
  10.7 8.6 all-to-all-start
  20.1 3.5 collective-permute-start.4
  25.6 3.6 collective-permute-start.6
  31.7 96.4 %all-to-all-done = bf16[16,80,1920]{2,1,0:T(8,128)(2,1)} async-done(((bf16[16,80,1920]{2,1,0:T(8,128)(2,1)}), bf16[16,80,1920]{2,1,0:T(8,128)(2,1)}, u32[]{:S(2)}, u32[]{:S(2)}) %all-to-all-start) | async-done | bytes 4915232 | tf_op jit(solution)/shard_map/all_to_all | solution.py:64
  128.0 4.0 convolution_convert_fusion
  145.4 3.6 collective-permute-start.2
  158.9 4.1 collective-permute-done.2
  164.2 9.0 %collective-permute-done.3 = bf16[256,1280]{1,0:T(8,128)(2,1)} collective-permute-done((bf16[256,1280]{1,0:T(8,128)(2,1)}, bf16[256,1280]{1,0:T(8,128)(2,1)}, u32[]{:S(2)}, u32[]{:S(2)}) %collective-permute-start.3) | collective-permute-done | bytes 655392 | tf_op jit(solution)/shard_map/ppermute | solution.py:16
  176.3 3.6 copy.25
  179.9 3.5 copy.26
  183.4 109.8 %while.32 = (s32[]{:T(128)}, bf16[10,256,64]{1,2,0:T(8,128)(2,1)}, bf16[10,256,64]{1,2,0:T(8,128)(2,1)}, f32[10,1280,64]{1,2,0:T(8,128)S(1)}, f32[10,1280,64]{1,...) while((s32[]{:T(128)}, bf16[10,256,64]{1,2,0:T(8,128)(2,1)}, ...), condition=%wide.region_6.7_spmd.clone, body=%wide.region_2.6_spmd.clone.sunk | while | flops 258637056 | bytes 10183041 | solution.py:143
  293.2 3.6 fusion.70
  301.0 6.0 collective-permute-start.11
  312.1 17.4 %collective-permute-done.10 = f32[256,1280]{0,1:T(8,128)S(1)} collective-permute-done((f32[256,1280]{0,1:T(8,128)S(1)}, f32[256,1280]{0,1:T(8,128)S(1)}, u32[]{:S(2)}, u32[]{:S(2)}) %collective-permute-start.10) | collective-permute-done | bytes 1310752 | tf_op jit(solution)/shard_map/ppermute | solution.py:16
  329.6 6.6 collective-permute-done.11
  336.2 9.0 %collective-permute-done.8 = f32[256,1280]{0,1:T(8,128)S(1)} collective-permute-done((f32[256,1280]{0,1:T(8,128)S(1)}, f32[256,1280]{0,1:T(8,128)S(1)}, u32[]{:S(2)}, u32[]{:S(2)}) %collective-permute-start.8) | collective-permute-done | bytes 1310752 | tf_op jit(solution)/shard_map/ppermute | solution.py:16
  345.2 7.0 collective-permute-done.9
  353.5 5.3 fusion.67
  358.9 127.6 %reduce-scatter.9.cloned.1.call-done = f32[640,80]{0,1:T(8,128)} async-done(((f32[640,1280]{0,1:T(8,128)}), f32[640,80]{0,1:T(8,128)}) %reduce-scatter.9.cloned.1.call-update) | async-done | bytes 204816 | tf_op jit(solution)/shard_map/reduce_scatter | solution.py:181
  487.8 153.5 %reduce-scatter.7.cloned.1.call-done = f32[1280,120]{0,1:T(8,128)} async-done(((f32[1280,1920]{0,1:T(8,128)}), f32[1280,120]{0,1:T(8,128)}) %reduce-scatter.7.cloned.1.call-update) | async-done | bytes 614416 | tf_op jit(solution)/shard_map/reduce_scatter | solution.py:180
  643.6 4.2 fusion.81
  649.2 146.3 %all-reduce.3.cloned.1.call-done = f32[640,80]{0,1:T(8,128)} async-done(((f32[640,80]{0,1:T(8,128)}), f32[640,80]{0,1:T(8,128)}) %all-reduce.3.cloned.1.call-update) | async-done | bytes 204816
  797.2 85.0 %reduce-scatter.11.cloned.1.call-done = f32[80,120]{1,0:T(8,128)} async-done(((f32[1280,120]{1,0:T(8,128)}), f32[80,120]{1,0:T(8,128)}) %reduce-scatter.11.cloned.1.call-update) | async-done | bytes 38416
  (173 shorter events, 160.2 us)
Async XLA Ops:
  10.7 117.3 %all-to-all-start = ((bf16[16,80,1920]{2,1,0:T(8,128)(2,1)}), bf16[16,80,1920]{2,1,0:T(8,128)(2,1)}, u32[]{:S(2)}, u32[]{:S(2)}) async-start(bf16[16,80,1920]{2,1,0:T(8,128)(2,1)} %stack.2), calls=%async_computation | async-start | bytes 9830400 | tf_op jit(solution)/shard_map/all_to_all | solution.py:64
  19.3 108.7 %copy-start.11 = (f32[1280]{0:T(1024)S(1)}, f32[1280]{0:T(1024)}, u32[]{:S(2)}) copy-start(f32[1280]{0:T(1024)} %param.34) | copy-start | bytes 15364
  19.3 121.0 %all-gather.2.cloned.1.call-start = ((), (), s32[]{:S(2)}) async-start(), calls=%async_computation.4 | async-start | bytes 1740800 | tf_op jit(solution)/shard_map/all_gather | solution.py:74
  20.1 466.4 %reduce-scatter.9.cloned.1.call-start = ((), (), s32[]{:S(2)}) async-start(), calls=%async_computation.6 | async-start | bytes 3481600 | tf_op jit(solution)/shard_map/reduce_scatter | solution.py:181
  20.1 117.3 %collective-permute-start.4 = (bf16[256]{0:T(256)(128)(2,1)S(1)}, bf16[256]{0:T(256)(128)(2,1)S(1)}, u32[]{:S(2)}, u32[]{:S(2)}) collective-permute-start(bf16[256]{0:T(256)(128)(2,1)S(1)} %convert_reduce_fusion.1), channel_id=1, source_target_pairs={{0,2},{1,3},{2,4},{3,5},{4,6},{5,7},{6,8},{7,9},{8,10},{9,11},{10,... | collective-permute-start | bytes 1544 | tf_op jit(solution)/shard_map/ppermute | solution.py:16
  23.6 114.1 %collective-permute-start.5 = (bf16[256]{0:T(256)(128)(2,1)S(1)}, bf16[256]{0:T(256)(128)(2,1)S(1)}, u32[]{:S(2)}, u32[]{:S(2)}) collective-permute-start(bf16[256]{0:T(256)(128)(2,1)S(1)} %convert_reduce_fusion.1), channel_id=1, source_target_pairs={{0,1},{1,2},{2,3},{3,4},{4,5},{5,6},{6,7},{7,8},{8,9},{9,10},{10,1... | collective-permute-start | bytes 1544 | tf_op jit(solution)/shard_map/ppermute | solution.py:16
  25.6 112.6 %collective-permute-start.6 = (bf16[256]{0:T(256)(128)(2,1)S(1)}, bf16[256]{0:T(256)(128)(2,1)S(1)}, u32[]{:S(2)}, u32[]{:S(2)}) collective-permute-start(bf16[256]{0:T(256)(128)(2,1)S(1)} %convert_reduce_fusion.1), channel_id=1, source_target_pairs={{1,0},{2,1},{3,2},{4,3},{5,4},{6,5},{7,6},{8,7},{9,8},{10,9},{11,1... | collective-permute-start | bytes 1544 | tf_op jit(solution)/shard_map/ppermute | solution.py:16
  29.2 109.2 %collective-permute-start.7 = (bf16[256]{0:T(256)(128)(2,1)S(1)}, bf16[256]{0:T(256)(128)(2,1)S(1)}, u32[]{:S(2)}, u32[]{:S(2)}) collective-permute-start(bf16[256]{0:T(256)(128)(2,1)S(1)} %convert_reduce_fusion.1), channel_id=1, source_target_pairs={{2,0},{3,1},{4,2},{5,3},{6,4},{7,5},{8,6},{9,7},{10,8},{11,9},{12,... | collective-permute-start | bytes 1544 | tf_op jit(solution)/shard_map/ppermute | solution.py:16
  133.9 20.6 %collective-permute-start = (bf16[256,1280]{1,0:T(8,128)(2,1)}, bf16[256,1280]{1,0:T(8,128)(2,1)}, u32[]{:S(2)}, u32[]{:S(2)}) collective-permute-start(bf16[256,1280]{1,0:T(8,128)(2,1)} %slice.121), channel_id=1, source_target_pairs={{0,2},{1,3},{2,4},{3,5},{4,6},{5,7},{6,8},{7,9},{8,10},{9,11},{10,... | collective-permute-start | bytes 1966088 | tf_op jit(solution)/shard_map/ppermute | solution.py:16
  138.4 19.4 %collective-permute-start.1 = (bf16[256,1280]{1,0:T(8,128)(2,1)}, bf16[256,1280]{1,0:T(8,128)(2,1)}, u32[]{:S(2)}, u32[]{:S(2)}) collective-permute-start(bf16[256,1280]{1,0:T(8,128)(2,1)} %slice.121), channel_id=1, source_target_pairs={{0,1},{1,2},{2,3},{3,4},{4,5},{5,6},{6,7},{7,8},{8,9},{9,10},{10,1... | collective-permute-start | bytes 1966088 | tf_op jit(solution)/shard_map/ppermute | solution.py:16
  145.4 17.7 %collective-permute-start.2 = (bf16[256,1280]{1,0:T(8,128)(2,1)}, bf16[256,1280]{1,0:T(8,128)(2,1)}, u32[]{:S(2)}, u32[]{:S(2)}) collective-permute-start(bf16[256,1280]{1,0:T(8,128)(2,1)} %slice.121), channel_id=1, source_target_pairs={{1,0},{2,1},{3,2},{4,3},{5,4},{6,5},{7,6},{8,7},{9,8},{10,9},{11,1... | collective-permute-start | bytes 1966088 | tf_op jit(solution)/shard_map/ppermute | solution.py:16
  149.0 24.2 %collective-permute-start.3 = (bf16[256,1280]{1,0:T(8,128)(2,1)}, bf16[256,1280]{1,0:T(8,128)(2,1)}, u32[]{:S(2)}, u32[]{:S(2)}) collective-permute-start(bf16[256,1280]{1,0:T(8,128)(2,1)} %slice.121), channel_id=1, source_target_pairs={{2,0},{3,1},{4,2},{5,3},{6,4},{7,5},{8,6},{9,7},{10,8},{11,9},{12,... | collective-permute-start | bytes 1966088 | tf_op jit(solution)/shard_map/ppermute | solution.py:16
  296.8 344.5 %reduce-scatter.7.cloned.1.call-start = ((), (), s32[]{:S(2)}) async-start(), calls=%async_computation.5 | async-start | bytes 10444800 | tf_op jit(solution)/shard_map/reduce_scatter | solution.py:180
  296.9 55.3 %copy-start = (f32[10,1280,64]{1,2,0:T(8,128)S(1)}, f32[10,1280,64]{1,2,0:T(8,128)}, u32[]{:S(2)}) copy-start(f32[10,1280,64]{1,2,0:T(8,128)} %get-tuple-element.301) | copy-start | bytes 9830404
  299.1 30.5 %collective-permute-start.10 = (f32[256,1280]{0,1:T(8,128)S(1)}, f32[256,1280]{0,1:T(8,128)S(1)}, u32[]{:S(2)}, u32[]{:S(2)}) collective-permute-start(f32[256,1280]{0,1:T(8,128)S(1)} %get-tuple-element.397), channel_id=1, source_target_pairs={{0,1},{1,2},{2,3},{3,4},{4,5},{5,6},{6,7},{7,8},{8,9},{9,10},{10,1... | collective-permute-start | bytes 3932168 | tf_op jit(solution)/shard_map/ppermute | solution.py:16
  301.0 35.2 %collective-permute-start.11 = (f32[256,1280]{0,1:T(8,128)S(1)}, f32[256,1280]{0,1:T(8,128)S(1)}, u32[]{:S(2)}, u32[]{:S(2)}) collective-permute-start(f32[256,1280]{0,1:T(8,128)S(1)} %get-tuple-element.396), channel_id=1, source_target_pairs={{0,2},{1,3},{2,4},{3,5},{4,6},{5,7},{6,8},{7,9},{8,10},{9,11},{10,... | collective-permute-start | bytes 3932168 | tf_op jit(solution)/shard_map/ppermute | solution.py:16
  307.1 38.1 %collective-permute-start.8 = (f32[256,1280]{0,1:T(8,128)S(1)}, f32[256,1280]{0,1:T(8,128)S(1)}, u32[]{:S(2)}, u32[]{:S(2)}) collective-permute-start(f32[256,1280]{0,1:T(8,128)S(1)} %get-tuple-element.394), channel_id=1, source_target_pairs={{2,0},{3,1},{4,2},{5,3},{6,4},{7,5},{8,6},{9,7},{10,8},{11,9},{12,... | collective-permute-start | bytes 3932168 | tf_op jit(solution)/shard_map/ppermute | solution.py:16
  309.0 43.2 %collective-permute-start.9 = (f32[256,1280]{0,1:T(8,128)S(1)}, f32[256,1280]{0,1:T(8,128)S(1)}, u32[]{:S(2)}, u32[]{:S(2)}) collective-permute-start(f32[256,1280]{0,1:T(8,128)S(1)} %get-tuple-element.395), channel_id=1, source_target_pairs={{1,0},{2,1},{3,2},{4,3},{5,4},{6,5},{7,6},{8,7},{9,8},{10,9},{11,1... | collective-permute-start | bytes 3932168 | tf_op jit(solution)/shard_map/ppermute | solution.py:16
  358.8 127.8 %copy-start.13 = (u32[256]{0:T(256)S(1)}, u32[256]{0:T(256)}, u32[]{:S(2)}) copy-start(u32[256]{0:T(256)} %constant.302) | copy-start | bytes 3076
  358.8 284.7 %copy-start.3 = (bf16[1,256,1280]{2,1,0:T(8,128)(2,1)S(1)}, bf16[1,256,1280]{2,1,0:T(8,128)(2,1)}, u32[]{:S(2)}) copy-start(bf16[1,256,1280]{2,1,0:T(8,128)(2,1)} %param.32) | copy-start | bytes 1966084
  358.8 284.7 %copy-start.7 = (bf16[256,1280]{0,1:T(8,128)(2,1)S(1)}, bf16[256,1280]{0,1:T(8,128)(2,1)}, u32[]{:S(2)}) copy-start(bf16[256,1280]{0,1:T(8,128)(2,1)} %copy-done.6) | copy-start | bytes 1966084
  358.9 284.7 %copy-start.10 = (bf16[10,256,64]{1,2,0:T(8,128)(2,1)S(1)}, bf16[10,256,64]{1,2,0:T(8,128)(2,1)}, u32[]{:S(2)}) copy-start(bf16[10,256,64]{1,2,0:T(8,128)(2,1)} %get-tuple-element.299) | copy-start | bytes 983044
  358.9 436.7 %all-reduce.3.cloned.1.call-start = ((), (), s32[]{:S(2)}) async-start(), calls=%async_computation.8 | async-start | bytes 409600
  486.5 395.6 %reduce-scatter.11.cloned.1.call-start = ((), (), s32[]{:S(2)}) async-start(), calls=%async_computation.7 | async-start | bytes 696320
  (8 other events, 129.3 us)
Sparse Core Ops, SparseCore 0:
  21.9 118.2 all-gather.1
  296.9 189.4 reduce-scatter.8
  491.3 150.0 reduce-scatter.6
  643.8 151.6 all-reduce.2
  797.9 84.2 reduce-scatter.10
